TPU v7x, 128 devices: a whole 4x4x4 slice. The times are simulated.
128 devices in a mesh: req: 4 (over z_lo, core), seq: 32 (over y, x, z_hi).
Axes of the slice: x: 4, y: 4, z: 4 (z_hi: 2, z_lo: 2; z = z_hi * 2 + z_lo), core: 2. Of those that a mesh axis runs over, the one named last changes fastest.
Arguments:
- prefill_query: bfloat16 [16384, 1536], P(('req', 'seq')), may hold values from -512 to 512
- prefill_key: bfloat16 [16384, 512], P(('req', 'seq')), may hold values from -512 to 512
- prefill_value: bfloat16 [16384, 512], P(('req', 'seq')), may hold values from -6 to 6
- prefill_resid: bfloat16 [16384, 1536], P(('req', 'seq')), may hold values from -6 to 6
- dec_query: bfloat16 [16, 1536], P('req'), may hold values from -512 to 512
- dec_key_new: bfloat16 [16, 512], P('req'), may hold values from -16 to 16
- dec_value_new: bfloat16 [16, 512], P('req'), may hold values from -6 to 6
- dec_resid: bfloat16 [16, 1536], P('req'), may hold values from -6 to 6
- cache_lengths: int32 [16], P('req'), may hold values from 16 to 32768, as said below
- key_cache: bfloat16 [16, 32768, 512], P('req', 'seq'), may hold values from -512 to 512
- value_cache: bfloat16 [16, 32768, 512], P('req', 'seq'), may hold values from -6 to 6
- attn_out_weight: bfloat16 [1536, 1536], replicated, may hold values from -0.15625 to 0.15625
- ffn_gain: float32 [1536], replicated, may hold values from 0.1 to 1.9
- expert_gate: bfloat16 [32, 1536, 512], P('seq', 'req'), may hold values from -0.15625 to 0.15625
- expert_up: bfloat16 [32, 1536, 512], P('seq', 'req'), may hold values from -0.15625 to 0.15625
- expert_down: bfloat16 [32, 512, 1536], P('seq', None, 'req'), may hold values from -0.25 to 0.25
- routes: int32 [16384, 8], P(('req', 'seq')), may hold values from 0 to 31, all different within a row; in each aligned block of 128 rows (0 to 127, 128 to 255, ...) at most 40 rows name the same one
- route_weights: float32 [16384, 8], P(('req', 'seq')), may hold values from 0.05 to 0.5
Outputs:
- prefill_out: bfloat16 [16384, 1536], P(('req', 'seq'))
- dec_out: bfloat16 [16, 1536], P('req')
Inputs may be any that keep to these rules, and one draw needn't show every extreme that they name: `routes`: in each aligned block of 128 rows (the rows of one device) no expert is named by more than 40 rows. `cache_lengths`: some request uses all 32768 positions.
All inputs are finite; a program needn't handle non-finite values.
Results may differ from a plain program's by a relative error of at most 0.012.
Values may be sent and summed in bfloat16 or wider, within the bound.
No kernel may reach another device: no remote copies, remote signals or barrier semaphores. Data moves between devices by JAX's collectives and lax.ppermute only.
A program may use at most 128 MiB of HBM per device.

v0:
```python
import math
import jax
import jax.numpy as jnp
from jax import lax
from jax.sharding import PartitionSpec as P

D = 1536
HEADS = 24
KVH = 8
HD = 64
EXPERTS = 32
CAP = 40
NEGATIVE = -1e30
EPSILON = 1e-05


def rms_scale(hidden, gain):
    values_float = hidden.astype(jnp.float32)
    mean_square = jnp.mean(values_float * values_float, axis=-1, keepdims=True)
    return (values_float * lax.rsqrt(mean_square + EPSILON) * gain).astype(jnp.bfloat16)


def per_request(function, operands):
    return jax.vmap(function)(operands)


def prefill_attention(prefill_query, prefill_key, prefill_value):
    token_rows = prefill_query.shape[0]
    group_size = HEADS // KVH
    score_scale = 1.0 / math.sqrt(HD)
    own_start = lax.axis_index("seq") * token_rows
    query_position = own_start + jnp.arange(token_rows, dtype=jnp.int32)
    query_heads = prefill_query.reshape(token_rows, KVH, group_size, HD)
    initial = (
        jnp.full((KVH, group_size, token_rows), NEGATIVE, jnp.float32),
        jnp.zeros((KVH, group_size, token_rows), jnp.float32),
        jnp.zeros((token_rows, KVH, group_size, HD), jnp.float32),
    )
    key_rows = lax.all_gather(prefill_key, "seq", axis=0, tiled=True)
    value_rows = lax.all_gather(prefill_value, "seq", axis=0, tiled=True)
    key_count = key_rows.shape[0]
    block_rows = 512
    key_heads = key_rows.reshape(key_count, KVH, HD)
    value_heads = value_rows.reshape(key_count, KVH, HD)

    def add_block(number, running_state):
        maxima, totals, weighted = running_state
        offset = number * block_rows
        key_block = lax.dynamic_slice_in_dim(key_heads, offset, block_rows, 0)
        value_block = lax.dynamic_slice_in_dim(value_heads, offset, block_rows, 0)
        key_position = offset + jnp.arange(block_rows, dtype=jnp.int32)
        visible = (key_position[None, :] <= query_position[:, None])[None, None, :, :]
        logits = (
            jnp.einsum("qkgd,pkd->kgqp", query_heads, key_block, preferred_element_type=jnp.float32)
            * score_scale
        )
        logits = jnp.where(visible, logits, NEGATIVE)
        new_maxima = jnp.maximum(maxima, jnp.max(logits, axis=-1))
        exponent = jnp.where(visible, jnp.exp(logits - new_maxima[..., None]), 0.0)
        rescale = jnp.exp(maxima - new_maxima)
        totals = totals * rescale + jnp.sum(exponent, axis=-1)
        weighted = weighted * jnp.moveaxis(rescale, 2, 0)[..., None] + jnp.einsum(
            "kgqp,pkd->qkgd",
            exponent.astype(jnp.bfloat16),
            value_block,
            preferred_element_type=jnp.float32,
        )
        return (new_maxima, totals, weighted)

    maxima, totals, weighted = lax.fori_loop(0, key_count // block_rows, add_block, initial)
    return (
        (weighted / jnp.moveaxis(totals, 2, 0)[..., None])
        .reshape(token_rows, HEADS * HD)
        .astype(jnp.bfloat16)
    )


def decode_attention(dec_query, dec_key_new, dec_value_new, cache_lengths, key_cache, value_cache):
    requests, block_length, feature_width = key_cache.shape
    group_size = HEADS // KVH
    score_scale = 1.0 / math.sqrt(HD)
    first_position = lax.axis_index("seq") * block_length
    positions = first_position + jnp.arange(block_length, dtype=jnp.int32)
    valid_mask = positions[None, :] < cache_lengths[:, None]
    query_heads = dec_query.reshape(requests, KVH, group_size, HD)
    key_heads = key_cache.reshape(requests, block_length, KVH, HD)
    value_heads = value_cache.reshape(requests, block_length, KVH, HD)

    def scores_of(pieces):
        query_one, keys_one, valid_one = pieces
        logits = (
            jnp.einsum("kgd,pkd->kgp", query_one, keys_one, preferred_element_type=jnp.float32)
            * score_scale
        )
        return jnp.where(valid_one[None, None, :], logits, NEGATIVE)

    def terms_of(pieces):
        scores_one, maxima_one, values_one, valid_one = pieces
        exponent = jnp.where(
            valid_one[None, None, :], jnp.exp(scores_one - maxima_one[..., None]), 0.0
        )
        weighted_one = jnp.einsum(
            "kgp,pkd->kgd",
            exponent.astype(jnp.bfloat16),
            values_one,
            preferred_element_type=jnp.float32,
        )
        return (jnp.sum(exponent, axis=-1), weighted_one)

    scores = per_request(scores_of, (query_heads, key_heads, valid_mask))
    local_maxima = jnp.max(scores, axis=-1)
    maxima = lax.pmax(local_maxima, "seq")
    totals, weighted = per_request(terms_of, (scores, maxima, value_heads, valid_mask))
    totals, weighted = lax.psum((totals, weighted), "seq")
    fresh_score = (
        jnp.einsum(
            "rkgd,rkd->rkg",
            query_heads,
            dec_key_new.reshape(requests, KVH, HD),
            preferred_element_type=jnp.float32,
        )
        * score_scale
    )
    final_maxima = jnp.maximum(maxima, fresh_score)
    rescale = jnp.exp(maxima - final_maxima)
    fresh_exp = jnp.exp(fresh_score - final_maxima)
    denominator = totals * rescale + fresh_exp
    fresh_weight = lax.optimization_barrier(fresh_exp.astype(jnp.bfloat16)).astype(jnp.float32)
    numerator = weighted * rescale[..., None] + fresh_weight[..., None] * dec_value_new.reshape(
        requests, KVH, 1, HD
    ).astype(jnp.float32)
    return (numerator / denominator[..., None]).reshape(requests, HEADS * HD).astype(jnp.bfloat16)


def expert_rows(rows_batch, gate_full, up_full, down_full):
    gate_value = jnp.einsum(
        "erd,edf->erf", rows_batch, gate_full, preferred_element_type=jnp.float32
    )
    up_value = jnp.einsum("erd,edf->erf", rows_batch, up_full, preferred_element_type=jnp.float32)
    hidden = (jax.nn.silu(gate_value) * up_value).astype(jnp.bfloat16)
    return jnp.einsum("erf,efd->erd", hidden, down_full, preferred_element_type=jnp.float32).astype(
        jnp.bfloat16
    )


def body(
    prefill_query,
    prefill_key,
    prefill_value,
    prefill_resid,
    dec_query,
    dec_key_new,
    dec_value_new,
    dec_resid,
    cache_lengths,
    key_cache,
    value_cache,
    attn_out_weight,
    ffn_gain,
    expert_gate,
    expert_up,
    expert_down,
    routes,
    route_weights,
):
    attended = prefill_attention(prefill_query, prefill_key, prefill_value)
    middle = (
        prefill_resid.astype(jnp.float32)
        + jnp.dot(attended, attn_out_weight, preferred_element_type=jnp.float32)
    ).astype(jnp.bfloat16)
    normed = rms_scale(middle, ffn_gain)
    gate_full, up_full = (
        lax.all_gather(expert_gate, "req", axis=1, tiled=True),
        lax.all_gather(expert_up, "req", axis=1, tiled=True),
    )
    down_full = lax.all_gather(expert_down, "req", axis=2, tiled=True)
    token_rows, top_count = routes.shape
    flat_expert = routes.reshape(-1)
    token_index = jnp.arange(token_rows * top_count, dtype=jnp.int32) // top_count
    onehot = (flat_expert[:, None] == jnp.arange(EXPERTS, dtype=jnp.int32)[None, :]).astype(
        jnp.int32
    )
    earlier = jnp.cumsum(onehot, axis=0) - onehot
    slot_index = jnp.sum(earlier * onehot, axis=1)
    outgoing = (
        jnp.zeros((EXPERTS, CAP, D), jnp.bfloat16)
        .at[flat_expert, slot_index]
        .set(normed[token_index])
    )
    incoming = lax.all_to_all(outgoing[:, None], "seq", split_axis=0, concat_axis=1, tiled=True)
    local_experts, sources, slot_count, feature_width = incoming.shape
    result = expert_rows(
        incoming.reshape(local_experts, sources * slot_count, feature_width),
        gate_full,
        up_full,
        down_full,
    )
    result = result.reshape(local_experts, sources, slot_count, feature_width)
    returned = lax.all_to_all(result, "seq", split_axis=1, concat_axis=0, tiled=True)
    picked = returned.reshape(EXPERTS, CAP, D)[flat_expert, slot_index]
    picked = picked.reshape(token_rows, top_count, D)
    mixture = jnp.sum(route_weights[..., None] * picked.astype(jnp.float32), axis=1)
    prefill_out = (middle.astype(jnp.float32) + mixture).astype(jnp.bfloat16)
    decoded = decode_attention(
        dec_query, dec_key_new, dec_value_new, cache_lengths, key_cache, value_cache
    )
    dec_out = (
        dec_resid.astype(jnp.float32)
        + jnp.dot(decoded, attn_out_weight, preferred_element_type=jnp.float32)
    ).astype(jnp.bfloat16)
    return (prefill_out, dec_out)


def solution(mesh):
    return jax.shard_map(
        body,
        mesh=mesh,
        in_specs=(
            P(("req", "seq"), None),
            P(("req", "seq"), None),
            P(("req", "seq"), None),
            P(("req", "seq"), None),
            P("req", None),
            P("req", None),
            P("req", None),
            P("req", None),
            P("req"),
            P("req", "seq", None),
            P("req", "seq", None),
            P(),
            P(),
            P("seq", "req", None),
            P("seq", "req", None),
            P("seq", None, "req"),
            P(("req", "seq"), None),
            P(("req", "seq"), None),
        ),
        out_specs=(P(("req", "seq"), None), P("req", None)),
        check_vma=False,
    )
```

profile of v0, /device:TPU:0, one launch (start us, length us, event | category | flops | bytes accessed | tf_op | source)
XLA Modules:
  0.0 821.3 jit_solution(3442623777327935929)
XLA Ops:
  11.1 1.2 copy.41
  12.3 9.0 %reduce-window.6 = s32[32,8,128]{2,1,0:T(8,128)S(1)} reduce-window(s32[32,8,128]{2,1,0:T(8,128)S(1)} %fusion.51, s32[]{:T(128)} %constant.93.clone.1), window={size=1x1x128 pad=0_0x0_0x127_0}, to_apply=%region_4.5 | reduce-window | flops 4161536 | bytes 262148 | tf_op jit(solution)/shard_map/reduce-window
  23.4 72.7 %all-gather.6.cloned.1.call-done = bf16[4096,512]{1,0:T(8,128)(2,1)} async-done(((bf16[128,512]{1,0:T(8,128)(2,1)}), bf16[4096,512]{1,0:T(8,128)(2,1)}) %all-gather.6.cloned.1.call-update) | async-done | bytes 4194320 | tf_op jit(solution)/shard_map/all_gather | solution.py:39
  96.1 6.4 copy.40
  102.5 75.9 %all-gather.8.cloned.1.call-done = bf16[4096,512]{1,0:T(8,128)(2,1)} async-done(((bf16[128,512]{1,0:T(8,128)(2,1)}), bf16[4096,512]{1,0:T(8,128)(2,1)}) %all-gather.8.cloned.1.call-update) | async-done | bytes 4194320 | tf_op jit(solution)/shard_map/all_gather | solution.py:40
  178.4 6.4 copy.42
  184.8 98.8 %while.18 = (s32[]{:T(128)}, f32[8,3,128]{2,1,0:T(4,128)S(1)}, f32[8,3,128]{2,1,0:T(4,128)S(1)}, f32[128,8,3,64]{0,3,2,1:T(8,128)S(1)}, bf16[4096,8,64]{0,2,1:T(...) while((s32[]{:T(128)}, f32[8,3,128]{2,1,0:T(4,128)S(1)}, ...), condition=%wide.region_3.4_spmd.clone, body=%wide.region_0.3_spmd.clone.sunk | while | flops 423774848 | bytes 47518944 | solution.py:70
  185.0 4.8 fusion.83
  189.8 4.5 fusion.85
  194.5 2.8 fusion.87
  197.5 4.8 fusion.83
  202.3 4.4 fusion.85
  206.9 2.8 fusion.87
  209.8 4.8 fusion.83
  214.6 4.4 fusion.85
  219.2 2.8 fusion.87
  222.2 4.8 fusion.83
  227.0 4.4 fusion.85
  231.6 2.8 fusion.87
  234.5 4.8 fusion.83
  239.3 4.4 fusion.85
  243.9 2.8 fusion.87
  246.8 4.8 fusion.83
  251.6 4.4 fusion.85
  256.2 2.8 fusion.87
  259.2 4.8 fusion.83
  263.9 4.4 fusion.85
  268.5 2.8 fusion.87
  271.5 4.8 fusion.83
  276.3 4.4 fusion.85
  280.8 2.8 fusion.87
  283.7 3.2 multiply_reduce_fusion
  287.0 0.9 copy-done.1
  288.0 18.6 %scatter_custom_fusion = bf16[1280,1536]{1,0:T(8,128)(2,1)} fusion(s32[1024]{0:T(1024)S(1)} %get-tuple-element.207, bf16[128,1536]{1,0:T(8,128)(2,1)S(1)} %multiply_convert_fusion, s32[1024]{0:T(1024)S(1)} %get-tuple-element.206, bf16[]{:T(256)} %constant.98.clone.1), kind=kCustom, calls=%fused_computation.36 | custom fusion | bytes 3932162
  306.7 5.1 all-to-all-start
  312.4 52.8 %all-to-all-done = bf16[32,1,40,1536]{3,2,1,0:T(8,128)(2,1)} async-done(((bf16[32,1,40,1536]{3,2,1,0:T(8,128)(2,1)}), bf16[32,1,40,1536]{3,2,1,0:T(8,128)(2,1)}, u32[]{:S(2)}, u32[]{:S(2)}) %all-to-all-start) | async-done | bytes 3932192 | tf_op jit(solution)/shard_map/all_to_all | solution.py:190
  365.2 4.8 fusion.36
  370.1 9.5 %convolution_convert_fusion = bf16[1280,1536]{1,0:T(8,128)(2,1)} fusion(bf16[1,512,1536]{2,1,0:T(8,128)(2,1)} %all-gather.14.cloned.1.call-done, bf16[1280,1536]{1,0:T(8,128)(2,1)} %bitcast.10, f32[1280,512]{1,0:T(8,128)S(1)} %fusion.36, bf16[1,1536,512]{2,1,0:T(8,128)(2,1)} %all-gather.12.cloned.1.call-done), kind=kOutput, calls=%fused_computation.32 | convolution fusion | flops 4032430080 | bytes 13631488 | tf_op jit(solution)/shard_map/erf,efd->erd/dot_general | solution.py:141
  379.5 7.5 all-to-all-start.1
  387.2 6.3 copy.51
  393.7 6.3 copy.50
  400.2 2.9 fusion.58
  403.2 205.7 %pmax.7 = f32[4,8,3]{2,1,0:T(8,128)S(1)} all-reduce(f32[4,8,3]{2,1,0:T(8,128)S(1)} %get-tuple-element.204), channel_id=1, replica_groups=mesh['req'=4,'seq'=32] {'seq'}, use_global_device_ids=true, to_apply=%region_11.12 | all-reduce | flops 96 | bytes 768 | tf_op jit(solution)/shard_map/pmax | solution.py:112
  609.3 3.5 fusion.43
  612.7 176.5 %all-reduce = (f32[4,8,3,64]{3,2,1,0:T(4,128)S(1)}, f32[4,8,3]{2,1,0:T(8,128)S(1)}) all-reduce(f32[4,8,3,64]{3,2,1,0:T(4,128)S(1)} %fusion.43, f32[4,8,3]{2,1,0:T(8,128)S(1)} %fusion.41), channel_id=1, replica_groups=mesh['req'=4,'seq'=32] {'seq'}, use_global_device_ids=true, to_apply=%region_12.13 | all-reduce | flops 6240 | bytes 49920 | tf_op jit(solution)/shard_map/psum | solution.py:114
  789.7 3.7 fusion.32
  793.4 17.8 %gather_fusion = bf16[1024,1536]{1,0:T(8,128)(2,1)S(1)} fusion(bf16[32,40,1536]{2,1,0:T(8,128)(2,1)} %bitcast.16, s32[1024]{0:T(1024)S(1)} %bitcast.111), kind=kCustom, calls=%fused_computation.1 | custom fusion | bytes 6299648 | tf_op jit(solution)/shard_map/gather | solution.py:200
  811.2 2.8 fusion.26
  (133 shorter events, 11.4 us)
Async XLA Ops:
  7.2 88.9 %all-gather.6.cloned.1.call-start = ((), (), s32[]{:S(2)}) async-start(), calls=%async_computation.2 | async-start | bytes 4325376 | tf_op jit(solution)/shard_map/all_gather | solution.py:39
  7.9 170.5 %all-gather.8.cloned.1.call-start = ((), (), s32[]{:S(2)}) async-start(), calls=%async_computation.3 | async-start | bytes 4325376 | tf_op jit(solution)/shard_map/all_gather | solution.py:40
  8.6 303.7 %all-gather.10.cloned.1.call-start = ((), (), s32[]{:S(2)}) async-start(), calls=%async_computation.4 | async-start | bytes 1966080 | tf_op jit(solution)/shard_map/all_gather | solution.py:173
  9.4 360.7 %all-gather.14.cloned.1.call-start = ((), (), s32[]{:S(2)}) async-start(), calls=%async_computation.6 | async-start | bytes 1966080 | tf_op jit(solution)/shard_map/all_gather | solution.py:176
  184.8 98.9 %copy-start.3 = (bf16[128,1536]{1,0:T(8,128)(2,1)S(1)}, bf16[128,1536]{1,0:T(8,128)(2,1)}, u32[]{:S(2)}) copy-start(bf16[128,1536]{1,0:T(8,128)(2,1)} %param.23) | copy-start | bytes 1179652
  189.8 4.7 copy-start
  202.3 4.6 copy-start
  214.6 4.6 copy-start
  227.0 4.6 copy-start
  239.3 4.6 copy-start
  251.6 4.6 copy-start
  263.9 4.6 copy-start
  276.2 4.6 copy-start
  283.6 4.3 copy-start.6
  287.0 0.9 copy-start.1
  306.7 58.5 %all-to-all-start = ((bf16[32,1,40,1536]{3,2,1,0:T(8,128)(2,1)}), bf16[32,1,40,1536]{3,2,1,0:T(8,128)(2,1)}, u32[]{:S(2)}, u32[]{:S(2)}) async-start(bf16[32,1,40,1536]{3,2,1,0:T(8,128)(2,1)} %bitcast.114), calls=%async_computation | async-start | bytes 7864320 | tf_op jit(solution)/shard_map/all_to_all | solution.py:190
  311.8 58.3 %all-gather.12.cloned.1.call-start = ((), (), s32[]{:S(2)}) async-start(), calls=%async_computation.5 | async-start | bytes 1966080 | tf_op jit(solution)/shard_map/all_gather | solution.py:174
  379.5 7.6 copy-start.7
  379.5 413.8 %all-to-all-start.1 = ((bf16[1,32,40,1536]{3,2,0,1:T(8,128)(2,1)}), bf16[1,32,40,1536]{3,2,0,1:T(8,128)(2,1)}, u32[]{:S(2)}, u32[]{:S(2)}) async-start(bf16[1,32,40,1536]{3,2,0,1:T(8,128)(2,1)} %bitcast.118), calls=%async_computation.1 | async-start | bytes 7864320 | tf_op jit(solution)/shard_map/all_to_all | solution.py:199
  387.2 6.3 copy-start.4
  393.6 6.4 copy-start.8
  393.6 6.4 copy-start.9
  393.7 6.5 copy-start.10
  403.2 386.5 %copy-start.5 = (bf16[4,1536]{1,0:T(4,128)(2,1)S(1)}, bf16[4,1536]{1,0:T(4,128)(2,1)}, u32[]{:S(2)}) copy-start(bf16[4,1536]{1,0:T(4,128)(2,1)} %param.27) | copy-start | bytes 36868
  811.2 2.8 copy-start.2
Sparse Core Ops, SparseCore 0:
  11.0 85.0 all-gather.5
  99.1 79.3 all-gather.7
  180.1 21.5 all-gather.9
  203.2 25.7 all-gather.13
  313.9 54.2 all-gather.11
where the time goes:
time: 823 us; the launch traced here: 821 us
  blocking collectives  382 us (46%)
  waiting for transfers between devices  204 us (25%)
  matrix products  88 us (11%)
  local copies, waits for them, and re-layouts  67 us (8%)
  other arithmetic  52 us (6%)
  between operations  14.1 us (2%)
  starting transfers between devices  13 us (2%)
    pmax x1, blocking collectives, decode_attention(): maxima = lax.pmax(local_maxima, 'seq')  206 us
    psum x1, blocking collectives, decode_attention(): totals, weighted = lax.psum((totals, weighted), 'seq')  176 us
    all_gather x1, waiting for transfers between devices, prefill_attention(): value_rows = lax.all_gather(prefill_value, 'seq', axis=0, tiled=True)  75.9 us
    all_gather x1, waiting for transfers between devices, prefill_attention(): key_rows = lax.all_gather(prefill_key, 'seq', axis=0, tiled=True)  72.7 us
    all_to_all x1, waiting for transfers between devices, body(): lax.all_to_all(outgoing[:, None], 'seq', split_axis=0, concat_axis=1, til...  52.8 us
    dot_general x8, matrix products, add_block(): jnp.einsum('qkgd,pkd->kgqp', query_heads, key_block, preferred_element_ty...  38.2 us
    reduce_sum x8, other arithmetic, add_block(): totals = totals * rescale + jnp.sum(exponent, axis=-1)  35.4 us
    unnamed x26, local copies, waits for them, and re-layouts  34.3 us
  transfers between devices with their start and end apart: 7, of which 3 were waited for; matrix products, arithmetic and copies ran while one was open for 21% of the time, Pallas kernels for 0%

commit v1 on v0

--- a/solution.py
+++ b/solution.py
@@ -3,6 +3,7 @@
 import jax.numpy as jnp
 from jax import lax
 from jax.sharding import PartitionSpec as P
+from jax.lax import all_gather
 
 D = 1536
 HEADS = 24
@@ -12,6 +13,14 @@
 CAP = 40
 NEGATIVE = -1e30
 EPSILON = 1e-05
+
+
+def make_group(own_rows, x0, bus_axis):
+    return jnp.split(
+        all_gather(jnp.concatenate([own_rows, x0], axis=1), bus_axis, axis=0, tiled=True),
+        [own_rows.shape[1]],
+        axis=1,
+    )
 
 
 def rms_scale(hidden, gain):
@@ -36,8 +45,7 @@
         jnp.zeros((KVH, group_size, token_rows), jnp.float32),
         jnp.zeros((token_rows, KVH, group_size, HD), jnp.float32),
     )
-    key_rows = lax.all_gather(prefill_key, "seq", axis=0, tiled=True)
-    value_rows = lax.all_gather(prefill_value, "seq", axis=0, tiled=True)
+    key_rows, value_rows = make_group(prefill_key, prefill_value, "seq")
     key_count = key_rows.shape[0]
     block_rows = 512
     key_heads = key_rows.reshape(key_count, KVH, HD)

time: 823 us -> 771 us (0.937)
  waiting for transfers between devices: 204 us -> 152 us
  other arithmetic: 52 us -> 30.3 us
  matrix products: 88 us -> 105 us
    all_gather x2 -> x1, waiting for transfers between devices: 149 us -> 95.4 us  [make_group(): all_gather(jnp.concatenate([own_rows, x0], axis=1), bus_axis, axis=0, til...]
    reduce_sum x8, other arithmetic: 35.4 us -> 11.8 us  [add_block(): totals = totals * rescale + jnp.sum(exponent, axis=-1)]
    split x0 -> x3, local copies, waits for them, and re-layouts: none -> 18.7 us  [make_group(): jnp.split(all_gather(jnp.concatenate([own_rows, x0], axis=1), bus_axis, a...]
    dot_general x8, matrix products: 22.1 us -> 39 us  [add_block(): jnp.einsum('kgqp,pkd->qkgd', exponent.astype(jnp.bfloat16), value_block,...]
    all_gather x2 -> x0, local copies, waits for them, and re-layouts: 12.8 us -> none  [the longest x1 6.43 us: prefill_attention(): key_rows = lax.all_gather(prefill_key, 'seq', axis=0, tiled=True)]
  transfers between devices with their start and end apart: 7 -> 6, of which waited for: 3 -> 2; matrix products, arithmetic and copies ran while one was open for 21% -> 23% of each run, Pallas kernels for 0% -> 0%
where the time goes in v1:
time: 771 us; the launch traced here: 769 us
  blocking collectives  383 us (50%)
  waiting for transfers between devices  152 us (20%)
  matrix products  105 us (14%)
  local copies, waits for them, and re-layouts  71.9 us (9%)
  other arithmetic  30.3 us (4%)
  between operations  14 us (2%)
  starting transfers between devices  11.8 us (2%)
    pmax x1, blocking collectives, decode_attention(): maxima = lax.pmax(local_maxima, 'seq')  207 us
    psum x1, blocking collectives, decode_attention(): totals, weighted = lax.psum((totals, weighted), 'seq')  176 us
    all_gather x1, waiting for transfers between devices, make_group(): all_gather(jnp.concatenate([own_rows, x0], axis=1), bus_axis, axis=0, til...  95.4 us
    all_to_all x1, waiting for transfers between devices, body(): lax.all_to_all(outgoing[:, None], 'seq', split_axis=0, concat_axis=1, til...  55.3 us
    dot_general x8, matrix products, add_block(): jnp.einsum('kgqp,pkd->qkgd', exponent.astype(jnp.bfloat16), value_block,...  39 us
    dot_general x8, matrix products, add_block(): jnp.einsum('qkgd,pkd->kgqp', query_heads, key_block, preferred_element_ty...  38.1 us
    unnamed x26, local copies, waits for them, and re-layouts  34.3 us
    split x3, local copies, waits for them, and re-layouts, make_group(): jnp.split(all_gather(jnp.concatenate([own_rows, x0], axis=1), bus_axis, a...  18.7 us
  transfers between devices with their start and end apart: 6, of which 2 were waited for; matrix products, arithmetic and copies ran while one was open for 23% of the time, Pallas kernels for 0%

profile of v1, /device:TPU:0, one launch (start us, length us, event | category | flops | bytes accessed | tf_op | source)
XLA Modules:
  0.0 769.1 jit_solution(16025975133880410723)
XLA Ops:
  7.2 1.7 pad_maximum_fusion
  11.6 9.0 %reduce-window.6 = s32[32,8,128]{2,1,0:T(8,128)S(1)} reduce-window(s32[32,8,128]{2,1,0:T(8,128)S(1)} %fusion.51, s32[]{:T(128)} %constant.93.clone.1), window={size=1x1x128 pad=0_0x0_0x127_0}, to_apply=%region_4.5 | reduce-window | flops 4161536 | bytes 262148 | tf_op jit(solution)/shard_map/reduce-window
  22.6 1.2 copy.41
  23.8 95.4 %all-gather.5.cloned.1.call-done = bf16[4096,1024]{1,0:T(8,128)(2,1)} async-done(((bf16[128,1024]{1,0:T(8,128)(2,1)}), bf16[4096,1024]{1,0:T(8,128)(2,1)}) %all-gather.5.cloned.1.call-update) | async-done | bytes 8388624 | tf_op jit(solution)/shard_map/all_gather | solution.py:20
  119.2 5.8 fusion.58
  125.0 6.4 copy.40
  131.5 6.5 copy.42
  138.0 91.1 %while.18 = (s32[]{:T(128)}, f32[8,3,128]{2,1,0:T(4,128)S(1)}, f32[8,3,128]{2,1,0:T(4,128)S(1)}, f32[128,8,3,64]{0,3,2,1:T(8,128)S(1)}, bf16[4096,8,64]{0,2,1:T(...) while((s32[]{:T(128)}, f32[8,3,128]{2,1,0:T(4,128)S(1)}, ...), condition=%wide.region_3.4_spmd.clone, body=%wide.region_0.3_spmd.clone.sunk | while | flops 423774848 | bytes 47518936 | solution.py:78
  138.1 4.8 fusion.84
  142.9 4.8 fusion.88
  147.8 1.5 fusion.86
  149.5 4.8 fusion.84
  154.3 5.1 fusion.88
  159.4 1.5 fusion.86
  161.1 4.8 fusion.84
  165.9 4.9 fusion.88
  170.8 1.5 fusion.86
  172.5 4.8 fusion.84
  177.3 4.8 fusion.88
  182.1 1.5 fusion.86
  183.8 4.8 fusion.84
  188.6 4.8 fusion.88
  193.5 1.5 fusion.86
  195.2 4.8 fusion.84
  200.0 4.8 fusion.88
  204.8 1.5 fusion.86
  206.5 4.8 fusion.84
  211.3 4.8 fusion.88
  216.2 1.5 fusion.86
  217.9 4.8 fusion.84
  222.6 4.8 fusion.88
  227.5 1.5 fusion.86
  229.1 3.2 multiply_reduce_fusion
  233.4 18.6 %scatter_custom_fusion = bf16[1280,1536]{1,0:T(8,128)(2,1)} fusion(s32[1024]{0:T(1024)S(1)} %get-tuple-element.209, bf16[128,1536]{1,0:T(8,128)(2,1)S(1)} %multiply_convert_fusion, s32[1024]{0:T(1024)S(1)} %get-tuple-element.208, bf16[]{:T(256)} %constant.98.clone.1), kind=kCustom, calls=%fused_computation.36 | custom fusion | bytes 3932162
  252.0 5.7 all-to-all-start
  258.3 55.3 %all-to-all-done = bf16[32,1,40,1536]{3,2,1,0:T(8,128)(2,1)} async-done(((bf16[32,1,40,1536]{3,2,1,0:T(8,128)(2,1)}), bf16[32,1,40,1536]{3,2,1,0:T(8,128)(2,1)}, u32[]{:S(2)}, u32[]{:S(2)}) %all-to-all-start) | async-done | bytes 3932192 | tf_op jit(solution)/shard_map/all_to_all | solution.py:198
  313.6 4.8 fusion.36
  318.5 9.4 %convolution_convert_fusion = bf16[1280,1536]{1,0:T(8,128)(2,1)} fusion(bf16[1,512,1536]{2,1,0:T(8,128)(2,1)} %all-gather.11.cloned.1.call-done, bf16[1280,1536]{1,0:T(8,128)(2,1)} %bitcast.10, f32[1280,512]{1,0:T(8,128)S(1)} %fusion.36, bf16[1,1536,512]{2,1,0:T(8,128)(2,1)} %all-gather.9.cloned.1.call-done), kind=kOutput, calls=%fused_computation.32 | convolution fusion | flops 4032430080 | bytes 13631488 | tf_op jit(solution)/shard_map/erf,efd->erd/dot_general | solution.py:149
  327.9 5.8 all-to-all-start.1
  333.7 6.3 copy.50
  340.1 6.4 copy.51
  346.6 2.9 fusion.59
  349.6 206.9 %pmax.7 = f32[4,8,3]{2,1,0:T(8,128)S(1)} all-reduce(f32[4,8,3]{2,1,0:T(8,128)S(1)} %get-tuple-element.206), channel_id=1, replica_groups=mesh['req'=4,'seq'=32] {'seq'}, use_global_device_ids=true, to_apply=%region_11.12 | all-reduce | flops 96 | bytes 768 | tf_op jit(solution)/shard_map/pmax | solution.py:120
  556.9 3.4 fusion.43
  560.3 176.5 %all-reduce = (f32[4,8,3,64]{3,2,1,0:T(4,128)S(1)}, f32[4,8,3]{2,1,0:T(8,128)S(1)}) all-reduce(f32[4,8,3,64]{3,2,1,0:T(4,128)S(1)} %fusion.43, f32[4,8,3]{2,1,0:T(8,128)S(1)} %fusion.41), channel_id=1, replica_groups=mesh['req'=4,'seq'=32] {'seq'}, use_global_device_ids=true, to_apply=%region_12.13 | all-reduce | flops 6240 | bytes 49920 | tf_op jit(solution)/shard_map/psum | solution.py:122
  737.4 3.7 fusion.32
  741.1 17.8 %gather_fusion = bf16[1024,1536]{1,0:T(8,128)(2,1)S(1)} fusion(bf16[32,40,1536]{2,1,0:T(8,128)(2,1)} %bitcast.16, s32[1024]{0:T(1024)S(1)} %bitcast.111), kind=kCustom, calls=%fused_computation.1 | custom fusion | bytes 6299648 | tf_op jit(solution)/shard_map/gather | solution.py:208
  758.9 2.8 fusion.26
  (132 shorter events, 10.0 us)
Async XLA Ops:
  7.2 112.1 %all-gather.5.cloned.1.call-start = ((), (), s32[]{:S(2)}) async-start(), calls=%async_computation.2 | async-start | bytes 8650752 | tf_op jit(solution)/shard_map/all_gather | solution.py:20
  8.9 249.4 %all-gather.7.cloned.1.call-start = ((), (), s32[]{:S(2)}) async-start(), calls=%async_computation.3 | async-start | bytes 1966080 | tf_op jit(solution)/shard_map/all_gather | solution.py:181
  9.7 308.7 %all-gather.11.cloned.1.call-start = ((), (), s32[]{:S(2)}) async-start(), calls=%async_computation.5 | async-start | bytes 1966080 | tf_op jit(solution)/shard_map/all_gather | solution.py:184
  138.0 91.2 %copy-start.3 = (bf16[128,1536]{1,0:T(8,128)(2,1)S(1)}, bf16[128,1536]{1,0:T(8,128)(2,1)}, u32[]{:S(2)}) copy-start(bf16[128,1536]{1,0:T(8,128)(2,1)} %param.23) | copy-start | bytes 1179652
  142.9 4.9 copy-start
  154.2 5.2 copy-start
  165.9 4.9 copy-start
  177.3 4.9 copy-start
  188.6 4.9 copy-start
  200.0 4.9 copy-start
  211.3 4.9 copy-start
  222.6 4.9 copy-start
  229.0 4.2 copy-start.6
  232.4 0.9 copy-start.1
  252.0 61.6 %all-to-all-start = ((bf16[32,1,40,1536]{3,2,1,0:T(8,128)(2,1)}), bf16[32,1,40,1536]{3,2,1,0:T(8,128)(2,1)}, u32[]{:S(2)}, u32[]{:S(2)}) async-start(bf16[32,1,40,1536]{3,2,1,0:T(8,128)(2,1)} %bitcast.114), calls=%async_computation | async-start | bytes 7864320 | tf_op jit(solution)/shard_map/all_to_all | solution.py:198
  257.7 60.7 %all-gather.9.cloned.1.call-start = ((), (), s32[]{:S(2)}) async-start(), calls=%async_computation.4 | async-start | bytes 1966080 | tf_op jit(solution)/shard_map/all_gather | solution.py:182
  327.9 5.8 copy-start.4
  327.9 413.2 %all-to-all-start.1 = ((bf16[1,32,40,1536]{3,2,0,1:T(8,128)(2,1)}), bf16[1,32,40,1536]{3,2,0,1:T(8,128)(2,1)}, u32[]{:S(2)}, u32[]{:S(2)}) async-start(bf16[1,32,40,1536]{3,2,0,1:T(8,128)(2,1)} %bitcast.118), calls=%async_computation.1 | async-start | bytes 7864320 | tf_op jit(solution)/shard_map/all_to_all | solution.py:207
  340.1 6.4 copy-start.7
  340.1 6.4 copy-start.10
  349.6 387.4 %copy-start.8 = (bf16[4,512]{1,0:T(4,128)(2,1)S(1)}, bf16[4,512]{1,0:T(4,128)(2,1)}, u32[]{:S(2)}) copy-start(bf16[4,512]{1,0:T(4,128)(2,1)} %param.26) | copy-start | bytes 12292
  349.6 387.8 %copy-start.9 = (f32[128,8]{0,1:T(8,128)S(1)}, f32[128,8]{0,1:T(8,128)}, u32[]{:S(2)}) copy-start(f32[128,8]{0,1:T(8,128)} %param.37) | copy-start | bytes 12292
  349.6 387.9 %copy-start.5 = (bf16[4,1536]{1,0:T(4,128)(2,1)S(1)}, bf16[4,1536]{1,0:T(4,128)(2,1)}, u32[]{:S(2)}) copy-start(bf16[4,1536]{1,0:T(4,128)(2,1)} %param.27) | copy-start | bytes 36868
  758.9 2.9 copy-start.2
Sparse Core Ops, SparseCore 0:
  11.6 107.5 all-gather.4
  120.9 22.4 all-gather.6
  145.1 25.7 all-gather.10
  259.9 54.0 all-gather.8
